TPU v7x, 32 devices: a whole 2x2x4 slice. The times are simulated.
32 devices in a mesh: phase: 4 (over x, core), seq: 4 (over z), mp: 2 (over y).
Axes of the slice: x: 2, y: 2, z: 4, core: 2. Of those that a mesh axis runs over, the one named last changes fastest.
Arguments:
- queries: bfloat16 [4, 2048, 4096], P('phase', 'seq', 'mp'), may hold values from -360 to 360
- key_weight: bfloat16 [4, 1024, 4096], P('phase', None, 'mp'), may hold values from -0.1875 to 0.1875
- value_weight: bfloat16 [4, 1024, 4096], P('phase', None, 'mp'), may hold values from -0.1875 to 0.1875
- enc_gain: float32 [1024], replicated, may hold values from 0.25 to 2
- neighbour_states: bfloat16 [80, 64, 1024], P('seq', ('phase', 'mp')), may hold values from -600 to 600
- slot_dest: int32 [80], P('seq'), may hold values from -1 to 63, as said below
Outputs:
- context: bfloat16 [4, 2048, 4096], P('phase', 'seq', 'mp')
Inputs may be any that keep to these rules, and one draw needn't show every extreme that they name: slot_dest names every position 0 to 63 exactly once and is -1 elsewhere. Positions 2 * 8 j to 2 * 8 (j + 1) - 1 belong to the tokens of index j of seq. The slots of one index of seq name at most 5 positions of any one index of seq, and this bound is reached; one index of seq has up to 20 filled slots, reached in every draw.
All inputs are finite; a program needn't handle non-finite values.
Results may differ from a plain program's by a relative error of at most 0.0074.
Values may be sent and summed in bfloat16 or wider, within the bound.
No kernel may reach another device: no remote copies, remote signals or barrier semaphores. Data moves between devices by JAX's collectives and lax.ppermute only.
A program may use at most 64 MiB of HBM per device.

v0:
```python
import functools
import math

import jax
import jax.numpy as jnp
from jax import lax
from jax.experimental import pallas as pl
from jax.experimental.pallas import tpu as pltpu
from jax.sharding import PartitionSpec as P


HD = 128
SEGLEN = 64
NEIGH = 2
LANES = 128
TILE = 8
EDGE = 16
FAR = 255.0
VMEM_LIMIT = 18 << 20
LAGS = (15, 30, 31)


def normalize(rows, gain):
    states = rows.astype(jnp.float32)
    meansq = jnp.mean(states * states, axis=-1, keepdims=True)
    return (states * lax.rsqrt(meansq + 1e-06) * gain).astype(jnp.bfloat16)


def pack_kernel(dest_hbm, place_ref, rows_hbm, gain_hbm, *refs, per_shard, capacity):
    parcels = refs[:-6]
    held, normed, dest_ref, rows_ref, gain_ref, sems = refs[-6:]
    shards = len(parcels)
    slots, tall, depth = rows_ref.shape
    feats = depth // LANES
    span = capacity * tall
    copies = [
        pltpu.make_async_copy(source, target, sems.at[index])
        for index, (source, target) in enumerate(
            ((rows_hbm, rows_ref), (gain_hbm, gain_ref), (dest_hbm, dest_ref))
        )
    ]
    for copy in copies:
        copy.start()
    held[...] = jnp.zeros_like(held)
    for copy in copies:
        copy.wait()
    normed[...] = normalize(rows_ref[...], gain_ref[...])
    lane = lax.broadcasted_iota(jnp.int32, (TILE, LANES), 1)
    counts = [jnp.int32(0)] * shards
    targets = [jnp.full((TILE, LANES), FAR, jnp.float32) for _ in range(shards)]
    for slot in range(slots):
        dest = dest_ref[slot]
        live = dest >= 0
        shard = jnp.where(live, dest, 0) // per_shard
        away = lax.rem(shard - place_ref[0] + shards, shards)
        away = jnp.where(live, away, shards)
        rank = jnp.int32(0)
        for other in range(shards):
            hit = away == other
            rank = jnp.where(hit, counts[other], rank)
            counts[other] = counts[other] + hit.astype(jnp.int32)
        index = away * capacity + rank
        for feat in range(feats):
            cols = slice(feat * LANES, (feat + 1) * LANES)
            held[index, feat * tall : (feat + 1) * tall, :] = normed[slot, :, cols]
        begin = rank * tall
        inside = (lane >= begin) & (lane < begin + tall)
        row = ((dest - shard * per_shard) * tall - begin + lane).astype(jnp.float32)
        for other in range(shards):
            targets[other] = jnp.where(inside & (away == other), row, targets[other])
    for shard in range(shards):
        for rank in range(capacity):
            begin = rank * feats * tall
            parcels[shard][begin : begin + feats * tall, :] = held[shard * capacity + rank]
        parcels[shard][feats * span :, :] = targets[shard].astype(jnp.bfloat16)


def pack(slot_dest, own, rows, gain, shards, per_shard, capacity):
    _, tall, depth = rows.shape
    size = depth // LANES * capacity * tall
    parcel = jax.ShapeDtypeStruct((size + TILE, LANES), jnp.bfloat16)
    return pl.pallas_call(
        functools.partial(pack_kernel, per_shard=per_shard, capacity=capacity),
        out_shape=[parcel] * shards,
        in_specs=[
            pl.BlockSpec(memory_space=pltpu.HBM),
            pl.BlockSpec(memory_space=pltpu.SMEM),
            pl.BlockSpec(memory_space=pltpu.HBM),
            pl.BlockSpec(memory_space=pltpu.HBM),
        ],
        out_specs=[pl.BlockSpec(memory_space=pltpu.VMEM)] * shards,
        scratch_shapes=[
            pltpu.VMEM((shards * capacity + 1, size // capacity, LANES), jnp.bfloat16),
            pltpu.VMEM(rows.shape, jnp.bfloat16),
            pltpu.SMEM(slot_dest.shape, jnp.int32),
            pltpu.VMEM(rows.shape, jnp.bfloat16),
            pltpu.VMEM((1, depth), jnp.float32),
            pltpu.SemaphoreType.DMA((3,)),
        ],
        compiler_params=pltpu.CompilerParams(vmem_limit_bytes=VMEM_LIMIT),
        name="pack",
    )(
        pltpu.with_memory_space_constraint(slot_dest, pltpu.HBM),
        own,
        pltpu.with_memory_space_constraint(rows, pltpu.HBM),
        pltpu.with_memory_space_constraint(gain.reshape(1, depth), pltpu.HBM),
    )


def unpack_kernel(*refs, tall):
    parcels, (block_ref, tail_ref) = refs[:-2], refs[-2:]
    rows, depth = block_ref.shape
    feats = depth // LANES
    span = (parcels[0].shape[0] - TILE) // feats
    place = lax.broadcasted_iota(jnp.int32, (rows, span), 0).astype(jnp.float32)
    picks = [
        (ref[feats * span :, :][:1, :span].astype(jnp.float32) == place).astype(jnp.bfloat16)
        for ref in parcels
    ]
    tail = tail_ref.shape[0]
    for feat in range(feats):
        total = jnp.zeros((rows, LANES), jnp.float32)
        for pick, ref in zip(picks, parcels):
            starts = range(feat * tall, feats * span, feats * tall)
            arrived = jnp.concatenate([ref[begin : begin + tall, :] for begin in starts], axis=0)
            total = total + jnp.dot(pick, arrived, preferred_element_type=jnp.float32)
        placed = total.astype(jnp.bfloat16)
        block_ref[:, feat * LANES : (feat + 1) * LANES] = placed
        tail_ref[:, feat * LANES : (feat + 1) * LANES] = placed[rows - tail :]


def unpack(parcels, depth, per_shard, tall):
    return pl.pallas_call(
        functools.partial(unpack_kernel, tall=tall),
        out_shape=[
            jax.ShapeDtypeStruct((per_shard * tall, depth), jnp.bfloat16),
            jax.ShapeDtypeStruct((NEIGH * tall, depth), jnp.bfloat16),
        ],
        compiler_params=pltpu.CompilerParams(vmem_limit_bytes=VMEM_LIMIT),
        name="unpack",
    )(*parcels)


def packing(slot_dest, shards, per_shard, capacity):
    count = slot_dest.shape[0]
    is_live = slot_dest >= 0
    target = jnp.where(is_live, slot_dest // per_shard, -1)
    order = jnp.arange(count)
    earlier = (target[:, None] == target[None, :]) & (order[None, :] < order[:, None])
    slot_rank = jnp.sum(earlier.astype(jnp.int32), axis=1)
    buffer_slot = jnp.where(is_live, target * capacity + slot_rank, -1)
    matches = jnp.arange(shards * capacity)[:, None] == buffer_slot[None, :]
    selector = matches.astype(jnp.bfloat16)
    sent_dest = jnp.sum(jnp.where(matches, slot_dest[None, :] + 1, 0), axis=1) - 1
    return selector, sent_dest.reshape(shards, capacity)


def select_rows(selector, rows):
    flattened = rows.reshape(rows.shape[0], -1)
    chosen = jnp.dot(selector, flattened, preferred_element_type=jnp.float32)
    return chosen.astype(jnp.bfloat16).reshape(selector.shape[0], *rows.shape[1:])


def route_plain(slot_dest, normed, own, shards, per_shard, capacity):
    selector, sent_dest = packing(slot_dest, shards, per_shard, capacity)
    sent = select_rows(selector, normed).reshape(shards, capacity, *normed.shape[1:])
    received = lax.all_to_all(sent, "seq", split_axis=0, concat_axis=0, tiled=True)
    received_dest = lax.all_to_all(sent_dest, "seq", split_axis=0, concat_axis=0, tiled=True)
    flat_dest = received_dest.reshape(-1)
    local = jnp.where(flat_dest >= 0, flat_dest - own * per_shard, -1)
    placer = (jnp.arange(per_shard)[:, None] == local[None, :]).astype(jnp.bfloat16)
    return select_rows(placer, received.reshape(shards * capacity, *normed.shape[1:]))


def hold_kernel(*refs):
    half = (len(refs) - 1) // 2
    sems = refs[-1]
    copies = [
        pltpu.make_async_copy(refs[index], refs[half + index], sems.at[index])
        for index in range(half)
    ]
    for copy in copies:
        copy.start()
    for copy in copies:
        copy.wait()


def hold(*arrays):
    return pl.pallas_call(
        hold_kernel,
        out_shape=[jax.ShapeDtypeStruct(array.shape, array.dtype) for array in arrays],
        in_specs=[pl.BlockSpec(memory_space=pltpu.HBM)] * len(arrays),
        out_specs=[pl.BlockSpec(memory_space=pltpu.VMEM)] * len(arrays),
        scratch_shapes=[pltpu.SemaphoreType.DMA((len(arrays),))],
        compiler_params=pltpu.CompilerParams(vmem_limit_bytes=VMEM_LIMIT),
        cost_estimate=pl.CostEstimate(
            flops=0, bytes_accessed=2 * sum(array.nbytes for array in arrays), transcendentals=0
        ),
        name="hold",
    )(*(pltpu.with_memory_space_constraint(array, pltpu.HBM) for array in arrays))


def resident(*arrays):
    return [pltpu.with_memory_space_constraint(array, pltpu.VMEM) for array in arrays]


def project_kernel(*refs, parts, stage, aliased, cols):
    blocks, (wk_ref, wv_ref) = refs[:parts], refs[parts : parts + 2]
    k_ref, v_ref, x_scr = refs[parts + (4 if aliased else 2) :]
    rows = blocks[0].shape[0]
    segs = k_ref.shape[1]
    tall = rows // segs
    base = stage * parts * tall
    for part in range(parts):
        x_scr[part * rows : (part + 1) * rows, :] = blocks[part][...]

    for step in range(wk_ref.shape[2] // cols):
        here = slice(step * cols, (step + 1) * cols)
        for w_ref, ref in ((wk_ref, k_ref), (wv_ref, v_ref)):
            out = jnp.dot(x_scr[...], w_ref[0, :, here], preferred_element_type=jnp.float32)
            out = out.astype(jnp.bfloat16)
            for part in range(parts):
                put = base + part * tall
                for seg in range(segs):
                    start = part * rows + seg * tall
                    for head in range(cols // HD):
                        ref[step * (cols // HD) + head, seg, put : put + tall, :] = out[
                            start : start + tall, head * HD : (head + 1) * HD
                        ]


def project(blocks, key_weight, value_weight, stage, stages, segs, carried=(), cols=512):
    parts = len(blocks)
    rows, depth = blocks[0].shape
    width = key_weight.shape[-1]
    keys = rows * parts // segs
    shape = jax.ShapeDtypeStruct((width // HD, segs, keys * stages, HD), jnp.bfloat16)
    vmem = pl.BlockSpec(memory_space=pltpu.VMEM)
    return pl.pallas_call(
        functools.partial(
            project_kernel, parts=parts, stage=stage, aliased=bool(carried), cols=cols
        ),
        out_shape=[shape, shape],
        in_specs=[vmem] * (parts + 2 + len(carried)),
        out_specs=[vmem, vmem],
        scratch_shapes=[pltpu.VMEM((rows * parts, depth), jnp.bfloat16)],
        input_output_aliases={parts + 2: 0, parts + 3: 1} if carried else {},
        compiler_params=pltpu.CompilerParams(vmem_limit_bytes=VMEM_LIMIT),
        cost_estimate=pl.CostEstimate(
            flops=4 * rows * parts * depth * width, bytes_accessed=0, transcendentals=0
        ),
        name="project",
    )(*blocks, *resident(key_weight, value_weight, *carried))


def attend_kernel(place_ref, *refs, counts, heads):
    mains, befores = counts
    blocks, refs = refs[: mains + befores], refs[mains + befores :]
    wk_ref, wv_ref, q_ref = refs[:3]
    kept = refs[3:-6]
    o_ref, x_scr, k_scr, v_scr, kb_scr, vb_scr = refs[-6:]
    count = k_scr.shape[0]
    rows = blocks[0].shape[0]
    tall = rows // count
    held = kept[0].shape[2] if kept else 0

    @pl.when(pl.program_id(0) == 0)
    def _():
        start = 0
        for ref in blocks:
            x_scr[start : start + ref.shape[0], :] = ref[...]
            start += ref.shape[0]

    width = heads * HD
    here = pl.ds(pl.multiple_of(pl.program_id(0) * width, width), width)
    for w_ref, scr, before_scr in ((wk_ref, k_scr, kb_scr), (wv_ref, v_scr, vb_scr)):
        w = w_ref[0, :, here] if kept else w_ref[0]
        out = jnp.dot(x_scr[...], w, preferred_element_type=jnp.float32)
        out = out.astype(jnp.bfloat16)
        for part in range(mains):
            for seg in range(count):
                start = part * rows + seg * tall
                put = held + part * tall
                scr[seg, put : put + tall, :] = out[start : start + tall]
        before_scr[...] = out[mains * rows :]

    for scr, ref in zip((k_scr, v_scr), kept):
        for head in range(heads):
            for seg in range(count):
                scr[seg, :held, head * HD : (head + 1) * HD] = ref[head, seg]

    def keys_of(which, seg, cols):
        if seg == 0:
            return (kb_scr, vb_scr)[which][:, cols]
        own = (k_scr, v_scr)[which][seg - 1, :, cols]
        return own

    scale = HD ** (-0.5) * math.log2(math.e)
    last = lax.broadcasted_iota(jnp.int32, (EDGE, 1), 0) == EDGE - 1
    whole = lax.broadcasted_iota(jnp.int32, (SEGLEN, 1), 0) == SEGLEN - 1
    heard = whole | (place_ref[1] == 0)

    def split(out, seg):
        return (out[:EDGE] if seg else None), out[EDGE if seg else 0 :]

    def join(outs, unit):
        lead, tail = outs[unit][1], outs[unit + 1][0]
        end = jnp.where(last, tail, lead[SEGLEN - EDGE :])
        return jnp.concatenate([lead[: SEGLEN - EDGE], end], axis=0)

    def score(head, seg):
        begin = SEGLEN * seg - (EDGE if seg else 0)
        end = SEGLEN * seg + (SEGLEN if seg < count else 0)
        out = lax.dot_general(
            q_ref[0, begin:end, head * HD : (head + 1) * HD],
            keys_of(0, seg, slice(head * HD, (head + 1) * HD)),
            (((1,), (1,)), ((), ())),
            preferred_element_type=jnp.float32,
        )
        return split(out, seg)

    def weigh(rows):
        top = jnp.max(rows, axis=-1, keepdims=True)
        exponent = jnp.exp2((rows - top) * scale)
        total = jnp.sum(exponent, axis=-1, keepdims=True)
        return (exponent * (1.0 / total)).astype(jnp.bfloat16)

    def gather(head, seg, unit):
        pieces = []
        if seg:
            pieces.append(weights[unit - 1][SEGLEN - EDGE :])
        if seg < count:
            pieces.append(weights[unit])
        lhs = jnp.concatenate(pieces, axis=0)
        values = keys_of(1, seg, slice(head * HD, (head + 1) * HD))
        return split(jnp.dot(lhs, values, preferred_element_type=jnp.float32), seg)

    units = [(head, seg) for head in range(heads) for seg in range(count + 1)]
    scores, weights, contexts = {}, {}, {}
    for turn in range(len(units) + LAGS[2]):
        if turn < len(units):
            scores[turn] = score(*units[turn])
        unit = turn - LAGS[0]
        if 0 <= unit < len(units) and units[unit][1] < count:
            weights[unit] = weigh(join(scores, unit))
        unit = turn - LAGS[1]
        if 0 <= unit < len(units):
            contexts[unit] = gather(*units[unit], unit)
        unit = turn - LAGS[2]
        if 0 <= unit < len(units) and units[unit][1] < count:
            head, block = units[unit]
            context = join(contexts, unit)
            if block == 0:
                context = jnp.where(heard, context, 0.0)
            span = slice(block * SEGLEN, (block + 1) * SEGLEN)
            o_ref[0, span, head * HD : (head + 1) * HD] = context.astype(jnp.bfloat16)


def attend(place, blocks, before, key_weight, value_weight, queries, kept=(), heads=4):
    depth = before[0].shape[1]
    _, tokens, width = queries.shape
    count = tokens // SEGLEN
    total = sum(block.shape[0] for block in blocks)
    halo = sum(block.shape[0] for block in before)
    cols = heads * HD
    column = lambda i, place: (0, 0, i)
    if kept:
        key_weight, value_weight, *kept = resident(key_weight, value_weight, *kept)
    held = kept[0].shape[2] if kept else 0
    late = pltpu.VMEM((count, held + total // count, cols), jnp.bfloat16)
    past = pltpu.VMEM((halo, cols), jnp.bfloat16)
    return pl.pallas_call(
        functools.partial(attend_kernel, counts=(len(blocks), len(before)), heads=heads),
        out_shape=jax.ShapeDtypeStruct(queries.shape, jnp.bfloat16),
        grid_spec=pltpu.PrefetchScalarGridSpec(
            num_scalar_prefetch=1,
            grid=(width // cols,),
            in_specs=[
                pl.BlockSpec(rows.shape, lambda i, place: (0, 0), pipeline_mode=pl.Buffered(1))
                for rows in (*blocks, *before)
            ]
            + [pl.BlockSpec(memory_space=pltpu.VMEM) if kept else pl.BlockSpec((1, depth, cols), column)] * 2
            + [pl.BlockSpec((1, tokens, cols), column)]
            + [
                pl.BlockSpec((heads, *rows.shape[1:]), lambda i, place: (i, 0, 0, 0))
                for rows in kept
            ],
            out_specs=pl.BlockSpec((1, tokens, cols), column),
            scratch_shapes=[
                pltpu.VMEM((total + halo, depth), jnp.bfloat16),
                late,
                late,
                past,
                past,
            ],
        ),
        compiler_params=pltpu.CompilerParams(
            dimension_semantics=("arbitrary",), vmem_limit_bytes=VMEM_LIMIT
        ),
        name="attend",
    )(place, *blocks, *before, key_weight, value_weight, queries, *kept)


def swap(rows, axes, sizes, move):
    pairs = []
    for phase in range(sizes[0]):
        for part in range(sizes[1]):
            to = move(phase, part)
            pairs.append((phase * sizes[1] + part, to[0] * sizes[1] + to[1]))
    return lax.ppermute(rows, axes, pairs)


def on_device_staged(place, block, tail, ahead, sizes, key_weight, value_weight, queries):
    axes = ("phase", "mp")
    core = lambda rows: swap(rows, axes, sizes, lambda p, m: (p ^ 1, m))
    x_even = lambda rows: swap(
        rows, axes, sizes, lambda p, m: (p ^ 2, m) if p % 2 == 0 else (p, m ^ 1)
    )
    y_even = lambda rows: swap(
        rows, axes, sizes, lambda p, m: (p ^ 2, m) if p % 2 else (p, m ^ 1)
    )
    segs = queries.shape[1] // SEGLEN

    over_a = y_even(block)
    over_b = x_even(block)
    beside = core(block)
    passed = lax.ppermute(tail, "seq", ahead)
    carried = project([block, beside], key_weight, value_weight, 0, 4, segs)
    corner = x_even(over_a)
    beside_a = core(over_a)
    beside_b = core(over_b)
    passed = jnp.concatenate([passed, y_even(passed)], axis=0)
    carried = project([over_a, over_b], key_weight, value_weight, 1, 4, segs, carried)
    passed = jnp.concatenate([passed, x_even(passed)], axis=0)
    before = core(passed)
    beside_corner = core(corner)
    carried = project([beside_a, beside_b], key_weight, value_weight, 2, 4, segs, carried)
    carried = project([corner, beside_corner], key_weight, value_weight, 3, 4, segs, carried)
    before = [passed, before]
    return attend(place, [], before, key_weight, value_weight, queries, carried)


def attention(queries, key_weight, value_weight, enc_gain, neighbour_states, slot_dest):
    shards = lax.axis_size("seq")
    sizes = (lax.axis_size("phase"), lax.axis_size("mp"))
    own = lax.axis_index("seq")
    tokens_here = queries.shape[1]
    per_shard = NEIGH * (tokens_here // SEGLEN)
    capacity = per_shard // shards + 1
    _, tall, depth = neighbour_states.shape
    ahead = [(i, i + 1) for i in range(shards - 1)]
    even = lax.axis_index("phase") & 1 ^ 1
    place = jnp.stack([own, jnp.where(own == 0, 1, 0), even]).astype(jnp.int32)
    if sizes == (4, 2) and tall % TILE == 0 and capacity * tall <= LANES:
        parcels = pack(
            slot_dest,
            place,
            neighbour_states,
            enc_gain,
            shards,
            per_shard,
            capacity,
        )
        key_weight, value_weight = hold(key_weight, value_weight)
        arrived = [parcels[0]]
        for away in range(1, shards):
            pairs = [(i, (i + away) % shards) for i in range(shards)]
            arrived.append(lax.ppermute(parcels[away], "seq", pairs))
        block, tail = unpack(arrived, depth, per_shard, tall)
        return on_device_staged(
            place, block, tail, ahead, sizes, key_weight, value_weight, queries
        )
    normed = normalize(neighbour_states, enc_gain)
    block = route_plain(slot_dest, normed, own, shards, per_shard, capacity)
    before = lax.ppermute(block[per_shard - NEIGH :], "seq", ahead)
    block = jnp.concatenate([block, before], axis=0)
    routed = lax.all_gather(block, ("phase", "mp"), axis=1, tiled=True)
    mine, before = routed[:per_shard], routed[per_shard:]
    return attend(
        place,
        [mine.reshape(-1, depth)],
        [before.reshape(-1, depth)],
        key_weight,
        value_weight,
        queries,
    )


def solution(mesh):
    in_specs = (
        P("phase", "seq", "mp"),
        P("phase", None, "mp"),
        P("phase", None, "mp"),
        P(),
        P("seq", ("phase", "mp"), None),
        P("seq"),
    )
    out_specs = P("phase", "seq", "mp")
    return jax.shard_map(
        attention, mesh=mesh, in_specs=in_specs, out_specs=out_specs, check_vma=False
    )
```

profile of v0, /device:TPU:0, one launch (start us, length us, event | category | flops | bytes accessed | tf_op | source)
XLA Modules:
  0.0 54.0 jit_solution(7517193620100877962)
XLA Ops:
  0.0 0.1 pad_add_fusion.place_ref
  0.1 1.9 %pack.1 = (bf16[328,128]{1,0:T(8,128)(2,1)S(1)}, bf16[328,128]{1,0:T(8,128)(2,1)S(1)}, bf16[328,128]{1,0:T(8,128)(2,1)S(1)}, bf16[328,128]{1,0:T(8,128)(2,1)S(1)}) custom-call(s32[20]{0:T(128)} %dest_hbm.1, s32[3]{0:T(128)S(1)} %pad_add_fusion.place_ref, bf16[20,8,1024]{2,1,0:T(8,128)(2,1)} %rows_hbm.1, f32[1,1024]{1,0:T(1,128)} %bitcast.4), custom_call_target="tpu_custom_call" | custom-call | tf_op jit(solution)/shard_map/pack/pallas_call | solution.py:82
  2.0 3.1 %collective-permute-start = (bf16[328,128]{1,0:T(8,128)(2,1)S(1)}, bf16[328,128]{1,0:T(8,128)(2,1)S(1)}, u32[]{:S(2)}, u32[]{:S(2)}) collective-permute-start(bf16[328,128]{1,0:T(8,128)(2,1)S(1)} %get-tuple-element.22), channel_id=1, source_target_pairs={{0,2},{2,4},{4,6},{6,0},{1,3},{3,5},{5,7},{7,1},{8,10},{10,12},{12... | collective-permute-start | bytes 251912 | tf_op jit(solution)/shard_map/ppermute | solution.py:468
  5.1 2.6 %collective-permute-start.1 = (bf16[328,128]{1,0:T(8,128)(2,1)S(1)}, bf16[328,128]{1,0:T(8,128)(2,1)S(1)}, u32[]{:S(2)}, u32[]{:S(2)}) collective-permute-start(bf16[328,128]{1,0:T(8,128)(2,1)S(1)} %get-tuple-element.23), channel_id=1, source_target_pairs={{0,4},{2,6},{4,0},{6,2},{1,5},{3,7},{5,1},{7,3},{8,12},{10,14},{12... | collective-permute-start | bytes 251912 | tf_op jit(solution)/shard_map/ppermute | solution.py:468
  7.7 1.3 %collective-permute-start.2 = (bf16[328,128]{1,0:T(8,128)(2,1)S(1)}, bf16[328,128]{1,0:T(8,128)(2,1)S(1)}, u32[]{:S(2)}, u32[]{:S(2)}) collective-permute-start(bf16[328,128]{1,0:T(8,128)(2,1)S(1)} %get-tuple-element.24), channel_id=1, source_target_pairs={{0,6},{2,0},{4,2},{6,4},{1,7},{3,1},{5,3},{7,5},{8,14},{10,8},{12,... | collective-permute-start | bytes 251912 | tf_op jit(solution)/shard_map/ppermute | solution.py:468
  9.1 1.1 %collective-permute-done.refs_1_ = bf16[328,128]{1,0:T(8,128)(2,1)S(1)} collective-permute-done((bf16[328,128]{1,0:T(8,128)(2,1)S(1)}, bf16[328,128]{1,0:T(8,128)(2,1)S(1)}, u32[]{:S(2)}, u32[]{:S(2)}) %collective-permute-start) | collective-permute-done | bytes 84000 | tf_op jit(solution)/shard_map/ppermute | solution.py:468
  10.2 3.1 %collective-permute-done.1.refs_2_ = bf16[328,128]{1,0:T(8,128)(2,1)S(1)} collective-permute-done((bf16[328,128]{1,0:T(8,128)(2,1)S(1)}, bf16[328,128]{1,0:T(8,128)(2,1)S(1)}, u32[]{:S(2)}, u32[]{:S(2)}) %collective-permute-start.1) | collective-permute-done | bytes 84000 | tf_op jit(solution)/shard_map/ppermute | solution.py:468
  13.3 0.2 collective-permute-done.2.refs_3_
  13.6 0.4 unpack.1
  14.0 3.9 %collective-permute-start.3 = (bf16[16,1024]{1,0:T(8,128)(2,1)S(1)}, bf16[16,1024]{1,0:T(8,128)(2,1)S(1)}, u32[]{:S(2)}, u32[]{:S(2)}) collective-permute-start(bf16[16,1024]{1,0:T(8,128)(2,1)S(1)} %get-tuple-element.25), channel_id=1, source_target_pairs={{0,2},{2,4},{4,6},{1,3},{3,5},{5,7},{8,10},{10,12},{12,14},{9,11},... | collective-permute-start | bytes 98312 | tf_op jit(solution)/shard_map/ppermute | solution.py:427
  17.9 3.5 %hold.1 = (bf16[1,1024,2048]{2,1,0:T(8,128)(2,1)S(1)}, bf16[1,1024,2048]{2,1,0:T(8,128)(2,1)S(1)}) custom-call(bf16[1,1024,2048]{2,1,0:T(8,128)(2,1)} %refs_0_.1, bf16[1,1024,2048]{2,1,0:T(8,128)(2,1)} %refs_1_.1), custom_call_target="tpu_custom_call" | custom-call | bytes 16777216 | tf_op jit(solution)/shard_map/hold/pallas_call | solution.py:189
  21.4 0.1 collective-permute-start.13
  21.5 1.6 %collective-permute-start.7 = (bf16[128,1024]{1,0:T(8,128)(2,1)S(1)}, bf16[128,1024]{1,0:T(8,128)(2,1)S(1)}, u32[]{:S(2)}, u32[]{:S(2)}) collective-permute-start(bf16[128,1024]{1,0:T(8,128)(2,1)S(1)} %get-tuple-element.28.refs_0_), channel_id=1, source_target_pairs={{0,1},{1,0},{8,24},{9,25},{16,17},{17,16},{24,8},{25,9},{2,3},{3,2... | collective-permute-start | bytes 786440 | tf_op jit(solution)/shard_map/ppermute | solution.py:410
  23.1 1.5 %collective-permute-start.11 = (bf16[128,1024]{1,0:T(8,128)(2,1)S(1)}, bf16[128,1024]{1,0:T(8,128)(2,1)S(1)}, u32[]{:S(2)}, u32[]{:S(2)}) collective-permute-start(bf16[128,1024]{1,0:T(8,128)(2,1)S(1)} %get-tuple-element.28.refs_0_), channel_id=1, source_target_pairs={{0,16},{1,17},{8,9},{9,8},{16,0},{17,1},{24,25},{25,24},{2,18},{3,... | collective-permute-start | bytes 786440 | tf_op jit(solution)/shard_map/ppermute | solution.py:410
  24.6 0.0 collective-permute-done.3
  24.6 0.5 collective-permute-start.4
  25.1 5.7 %collective-permute-done.4 = bf16[16,1024]{1,0:T(8,128)(2,1)S(1)} collective-permute-done((bf16[16,1024]{1,0:T(8,128)(2,1)S(1)}, bf16[16,1024]{1,0:T(8,128)(2,1)S(1)}, u32[]{:S(2)}, u32[]{:S(2)}) %collective-permute-start.4) | collective-permute-done | bytes 32800 | tf_op jit(solution)/shard_map/ppermute | solution.py:410
  30.8 1.5 %collective-permute-start.5 = (bf16[32,1024]{1,0:T(8,128)(2,1)S(1)}, bf16[32,1024]{1,0:T(8,128)(2,1)S(1)}, u32[]{:S(2)}, u32[]{:S(2)}) collective-permute-start(bf16[32,1024]{1,0:T(8,128)(2,1)S(1)} %pad_maximum_fusion), channel_id=1, source_target_pairs={{0,16},{1,17},{8,9},{9,8},{16,0},{17,1},{24,25},{25,24},{2,18},{3,... | collective-permute-start | bytes 196616 | tf_op jit(solution)/shard_map/ppermute | solution.py:410
  32.3 0.0 collective-permute-done.7.refs_0_
  32.3 0.5 collective-permute-start.8
  32.8 2.2 %collective-permute-done.5 = bf16[32,1024]{1,0:T(8,128)(2,1)S(1)} collective-permute-done((bf16[32,1024]{1,0:T(8,128)(2,1)S(1)}, bf16[32,1024]{1,0:T(8,128)(2,1)S(1)}, u32[]{:S(2)}, u32[]{:S(2)}) %collective-permute-start.5) | collective-permute-done | bytes 65568 | tf_op jit(solution)/shard_map/ppermute | solution.py:410
  35.1 0.0 collective-permute-start.6
  35.1 0.5 collective-permute-start.10
  35.6 0.0 collective-permute-done.11.refs_1_
  35.6 0.1 collective-permute-start.12
  35.6 0.0 collective-permute-done.13.refs_1_
  35.6 2.4 %project.4 = (bf16[16,8,128,128]{3,2,1,0:T(8,128)(2,1)S(1)}, bf16[16,8,128,128]{3,2,1,0:T(8,128)(2,1)S(1)}) custom-call(bf16[128,1024]{1,0:T(8,128)(2,1)S(1)} %get-tuple-element.28.refs_0_, bf16[128,1024]{1,0:T(8,128)(2,1)S(1)} %collective-permute-done.13.refs_1_, bf16[1,1024,2048]{2,1,0:T(8,128)(2,1)S(1)} %get-tuple-element.26.refs_2_, ...), custom_call_target="tpu_custom_call" | custom-call | flops 2147483648 | tf_op jit(solution)/shard_map/project/pallas_call | solution.py:239
  38.0 0.7 %collective-permute-done.8.refs_0_ = bf16[128,1024]{1,0:T(8,128)(2,1)S(1)} collective-permute-done((bf16[128,1024]{1,0:T(8,128)(2,1)S(1)}, bf16[128,1024]{1,0:T(8,128)(2,1)S(1)}, u32[]{:S(2)}, u32[]{:S(2)}) %collective-permute-start.8) | collective-permute-done | bytes 262176 | tf_op jit(solution)/shard_map/ppermute | solution.py:410
  38.7 0.0 collective-permute-start.9
  38.7 2.4 %project.5 = (bf16[16,8,128,128]{3,2,1,0:T(8,128)(2,1)S(1)}, bf16[16,8,128,128]{3,2,1,0:T(8,128)(2,1)S(1)}) custom-call(bf16[128,1024]{1,0:T(8,128)(2,1)S(1)} %collective-permute-done.7.refs_0_, bf16[128,1024]{1,0:T(8,128)(2,1)S(1)} %collective-permute-done.11.refs_1_, ...), custom_call_target="tpu_custom_call", output_to_operand_aliasing={{0}: (4, {}), {1}: (5, {})} | custom-call | flops 2147483648 | tf_op jit(solution)/shard_map/project/pallas_call | solution.py:239
  41.1 0.0 collective-permute-done.10.refs_0_
  41.1 0.0 collective-permute-done.12.refs_1_
  41.1 2.4 %project.6 = (bf16[16,8,128,128]{3,2,1,0:T(8,128)(2,1)S(1)}, bf16[16,8,128,128]{3,2,1,0:T(8,128)(2,1)S(1)}) custom-call(bf16[128,1024]{1,0:T(8,128)(2,1)S(1)} %collective-permute-done.10.refs_0_, bf16[128,1024]{1,0:T(8,128)(2,1)S(1)} %collective-permute-done.12.refs_1_, ...), custom_call_target="tpu_custom_call", output_to_operand_aliasing={{0}: (4, {}), {1}: (5, {})} | custom-call | flops 2147483648 | tf_op jit(solution)/shard_map/project/pallas_call | solution.py:239
  43.5 0.0 collective-permute-done.9.refs_1_
  43.5 0.0 copy-start
  43.5 2.4 %project.7 = (bf16[16,8,128,128]{3,2,1,0:T(8,128)(2,1)S(1)}, bf16[16,8,128,128]{3,2,1,0:T(8,128)(2,1)S(1)}) custom-call(bf16[128,1024]{1,0:T(8,128)(2,1)S(1)} %collective-permute-done.8.refs_0_, bf16[128,1024]{1,0:T(8,128)(2,1)S(1)} %collective-permute-done.9.refs_1_, ...), custom_call_target="tpu_custom_call", output_to_operand_aliasing={{0}: (4, {}), {1}: (5, {})} | custom-call | flops 2147483648 | tf_op jit(solution)/shard_map/project/pallas_call | solution.py:239
  45.9 0.0 collective-permute-done.6.refs_1_
  45.9 0.0 copy-done
  45.9 8.1 %attend.1 = bf16[1,512,2048]{2,1,0:T(8,128)(2,1)} custom-call(s32[3]{0:T(128)S(1)} %pad_add_fusion.place_ref, bf16[64,1024]{1,0:T(8,128)(2,1)S(1)} %constant_dynamic-update-slice_fusion.refs_0_, bf16[64,1024]{1,0:T(8,128)(2,1)S(1)} %collective-permute-done.6.refs_1_, bf16[1,1024,2048]{2,1,0:T(8,128)(2,1)S(1)} %get-tuple-element.26.refs_2_, ...), custom_call_target="tpu_custom_call" | custom-call | tf_op jit(solution)/shard_map/attend/pallas_call | solution.py:372
  (4 shorter events, 0.0 us)
Async XLA Ops:
  2.0 8.2 %collective-permute-start = (bf16[328,128]{1,0:T(8,128)(2,1)S(1)}, bf16[328,128]{1,0:T(8,128)(2,1)S(1)}, u32[]{:S(2)}, u32[]{:S(2)}) collective-permute-start(bf16[328,128]{1,0:T(8,128)(2,1)S(1)} %get-tuple-element.22), channel_id=1, source_target_pairs={{0,2},{2,4},{4,6},{6,0},{1,3},{3,5},{5,7},{7,1},{8,10},{10,12},{12... | collective-permute-start | bytes 251912 | tf_op jit(solution)/shard_map/ppermute | solution.py:468
  5.1 8.2 %collective-permute-start.1 = (bf16[328,128]{1,0:T(8,128)(2,1)S(1)}, bf16[328,128]{1,0:T(8,128)(2,1)S(1)}, u32[]{:S(2)}, u32[]{:S(2)}) collective-permute-start(bf16[328,128]{1,0:T(8,128)(2,1)S(1)} %get-tuple-element.23), channel_id=1, source_target_pairs={{0,4},{2,6},{4,0},{6,2},{1,5},{3,7},{5,1},{7,3},{8,12},{10,14},{12... | collective-permute-start | bytes 251912 | tf_op jit(solution)/shard_map/ppermute | solution.py:468
  7.7 5.9 %collective-permute-start.2 = (bf16[328,128]{1,0:T(8,128)(2,1)S(1)}, bf16[328,128]{1,0:T(8,128)(2,1)S(1)}, u32[]{:S(2)}, u32[]{:S(2)}) collective-permute-start(bf16[328,128]{1,0:T(8,128)(2,1)S(1)} %get-tuple-element.24), channel_id=1, source_target_pairs={{0,6},{2,0},{4,2},{6,4},{1,7},{3,1},{5,3},{7,5},{8,14},{10,8},{12,... | collective-permute-start | bytes 251912 | tf_op jit(solution)/shard_map/ppermute | solution.py:468
  14.0 10.6 %collective-permute-start.3 = (bf16[16,1024]{1,0:T(8,128)(2,1)S(1)}, bf16[16,1024]{1,0:T(8,128)(2,1)S(1)}, u32[]{:S(2)}, u32[]{:S(2)}) collective-permute-start(bf16[16,1024]{1,0:T(8,128)(2,1)S(1)} %get-tuple-element.25), channel_id=1, source_target_pairs={{0,2},{2,4},{4,6},{1,3},{3,5},{5,7},{8,10},{10,12},{12,14},{9,11},... | collective-permute-start | bytes 98312 | tf_op jit(solution)/shard_map/ppermute | solution.py:427
  21.4 14.2 %collective-permute-start.13 = (bf16[128,1024]{1,0:T(8,128)(2,1)S(1)}, bf16[128,1024]{1,0:T(8,128)(2,1)S(1)}, u32[]{:S(2)}, u32[]{:S(2)}) collective-permute-start(bf16[128,1024]{1,0:T(8,128)(2,1)S(1)} %get-tuple-element.28.refs_0_), channel_id=1, source_target_pairs={{0,8},{1,9},{8,0},{9,1},{16,24},{17,25},{24,16},{25,17},{2,10},{3,... | collective-permute-start | bytes 786440 | tf_op jit(solution)/shard_map/ppermute | solution.py:410
  21.5 10.8 %collective-permute-start.7 = (bf16[128,1024]{1,0:T(8,128)(2,1)S(1)}, bf16[128,1024]{1,0:T(8,128)(2,1)S(1)}, u32[]{:S(2)}, u32[]{:S(2)}) collective-permute-start(bf16[128,1024]{1,0:T(8,128)(2,1)S(1)} %get-tuple-element.28.refs_0_), channel_id=1, source_target_pairs={{0,1},{1,0},{8,24},{9,25},{16,17},{17,16},{24,8},{25,9},{2,3},{3,2... | collective-permute-start | bytes 786440 | tf_op jit(solution)/shard_map/ppermute | solution.py:410
  23.1 12.5 %collective-permute-start.11 = (bf16[128,1024]{1,0:T(8,128)(2,1)S(1)}, bf16[128,1024]{1,0:T(8,128)(2,1)S(1)}, u32[]{:S(2)}, u32[]{:S(2)}) collective-permute-start(bf16[128,1024]{1,0:T(8,128)(2,1)S(1)} %get-tuple-element.28.refs_0_), channel_id=1, source_target_pairs={{0,16},{1,17},{8,9},{9,8},{16,0},{17,1},{24,25},{25,24},{2,18},{3,... | collective-permute-start | bytes 786440 | tf_op jit(solution)/shard_map/ppermute | solution.py:410
  24.6 6.2 %collective-permute-start.4 = (bf16[16,1024]{1,0:T(8,128)(2,1)S(1)}, bf16[16,1024]{1,0:T(8,128)(2,1)S(1)}, u32[]{:S(2)}, u32[]{:S(2)}) collective-permute-start(bf16[16,1024]{1,0:T(8,128)(2,1)S(1)} %collective-permute-done.3), channel_id=1, source_target_pairs={{0,1},{1,0},{8,24},{9,25},{16,17},{17,16},{24,8},{25,9},{2,3},{3,2... | collective-permute-start | bytes 98312 | tf_op jit(solution)/shard_map/ppermute | solution.py:410
  30.8 4.3 %collective-permute-start.5 = (bf16[32,1024]{1,0:T(8,128)(2,1)S(1)}, bf16[32,1024]{1,0:T(8,128)(2,1)S(1)}, u32[]{:S(2)}, u32[]{:S(2)}) collective-permute-start(bf16[32,1024]{1,0:T(8,128)(2,1)S(1)} %pad_maximum_fusion), channel_id=1, source_target_pairs={{0,16},{1,17},{8,9},{9,8},{16,0},{17,1},{24,25},{25,24},{2,18},{3,... | collective-permute-start | bytes 196616 | tf_op jit(solution)/shard_map/ppermute | solution.py:410
  32.3 6.4 %collective-permute-start.8 = (bf16[128,1024]{1,0:T(8,128)(2,1)S(1)}, bf16[128,1024]{1,0:T(8,128)(2,1)S(1)}, u32[]{:S(2)}, u32[]{:S(2)}) collective-permute-start(bf16[128,1024]{1,0:T(8,128)(2,1)S(1)} %collective-permute-done.7.refs_0_), channel_id=1, source_target_pairs={{0,16},{1,17},{8,9},{9,8},{16,0},{17,1},{24,25},{25,24},{2,18},{3,... | collective-permute-start | bytes 786440 | tf_op jit(solution)/shard_map/ppermute | solution.py:410
  35.1 10.8 %collective-permute-start.6 = (bf16[64,1024]{1,0:T(8,128)(2,1)S(1)}, bf16[64,1024]{1,0:T(8,128)(2,1)S(1)}, u32[]{:S(2)}, u32[]{:S(2)}) collective-permute-start(bf16[64,1024]{1,0:T(8,128)(2,1)S(1)} %constant_dynamic-update-slice_fusion.refs_0_), channel_id=1, source_target_pairs={{0,8},{1,9},{8,0},{9,1},{16,24},{17,25},{24,16},{25,17},{2,10},{3,... | collective-permute-start | bytes 393224 | tf_op jit(solution)/shard_map/ppermute | solution.py:410
  35.1 6.0 %collective-permute-start.10 = (bf16[128,1024]{1,0:T(8,128)(2,1)S(1)}, bf16[128,1024]{1,0:T(8,128)(2,1)S(1)}, u32[]{:S(2)}, u32[]{:S(2)}) collective-permute-start(bf16[128,1024]{1,0:T(8,128)(2,1)S(1)} %collective-permute-done.7.refs_0_), channel_id=1, source_target_pairs={{0,8},{1,9},{8,0},{9,1},{16,24},{17,25},{24,16},{25,17},{2,10},{3,... | collective-permute-start | bytes 786440 | tf_op jit(solution)/shard_map/ppermute | solution.py:410
  35.6 5.5 %collective-permute-start.12 = (bf16[128,1024]{1,0:T(8,128)(2,1)S(1)}, bf16[128,1024]{1,0:T(8,128)(2,1)S(1)}, u32[]{:S(2)}, u32[]{:S(2)}) collective-permute-start(bf16[128,1024]{1,0:T(8,128)(2,1)S(1)} %collective-permute-done.11.refs_1_), channel_id=1, source_target_pairs={{0,8},{1,9},{8,0},{9,1},{16,24},{17,25},{24,16},{25,17},{2,10},{3,... | collective-permute-start | bytes 786440 | tf_op jit(solution)/shard_map/ppermute | solution.py:410
  38.7 4.8 %collective-permute-start.9 = (bf16[128,1024]{1,0:T(8,128)(2,1)S(1)}, bf16[128,1024]{1,0:T(8,128)(2,1)S(1)}, u32[]{:S(2)}, u32[]{:S(2)}) collective-permute-start(bf16[128,1024]{1,0:T(8,128)(2,1)S(1)} %collective-permute-done.8.refs_0_), channel_id=1, source_target_pairs={{0,8},{1,9},{8,0},{9,1},{16,24},{17,25},{24,16},{25,17},{2,10},{3,... | collective-permute-start | bytes 786440 | tf_op jit(solution)/shard_map/ppermute | solution.py:410
  43.5 2.4 %copy-start = (bf16[1,512,2048]{2,1,0:T(8,128)(2,1)S(1)}, bf16[1,512,2048]{2,1,0:T(8,128)(2,1)}, u32[]{:S(2)}) copy-start(bf16[1,512,2048]{2,1,0:T(8,128)(2,1)} %refs_4_.1) | copy-start | bytes 6291460
where the time goes:
time: 54.2 us; the launch traced here: 54 us
  Pallas kernels  23.4 us (43%)
  starting transfers between devices  17.2 us (32%)
  waiting for transfers between devices  13.1 us (24%)
    pallas_call x4, Pallas kernels, project(): pl.pallas_call(functools.partial(project_kernel, parts=parts, stage=stage...  9.49 us
    ppermute x10, waiting for transfers between devices, swap(): return lax.ppermute(rows, axes, pairs)  8.6 us
    pallas_call x1, Pallas kernels, attend(): pl.pallas_call(functools.partial(attend_kernel, counts=(len(blocks), len(...  8.11 us
    ppermute x3, starting transfers between devices, attention(): arrived.append(lax.ppermute(parcels[away], 'seq', pairs))  7.04 us
    ppermute x10, starting transfers between devices, swap(): return lax.ppermute(rows, axes, pairs)  6.26 us
    ppermute x3, waiting for transfers between devices, attention(): arrived.append(lax.ppermute(parcels[away], 'seq', pairs))  4.51 us
    ppermute x1, starting transfers between devices, on_device_staged(): passed = lax.ppermute(tail, 'seq', ahead)  3.93 us
    pallas_call x1, Pallas kernels, hold(): pl.pallas_call(hold_kernel, out_shape=[jax.ShapeDtypeStruct(array.shape,...  3.49 us
  transfers between devices with their start and end apart: 14, of which 6 were waited for; matrix products, arithmetic and copies ran while one was open for 0% of the time, Pallas kernels for 24%

commit v1 on v0

--- a/solution.py
+++ b/solution.py
@@ -284,10 +284,10 @@
                 scr[seg, put : put + tall, :] = out[start : start + tall]
         before_scr[...] = out[mains * rows :]
 
-    for scr, ref in zip((k_scr, v_scr), kept):
-        for head in range(heads):
-            for seg in range(count):
-                scr[seg, :held, head * HD : (head + 1) * HD] = ref[head, seg]
+    def settle(which, head, seg):
+        if kept and seg:
+            scr = (k_scr, v_scr)[which]
+            scr[seg - 1, :held, head * HD : (head + 1) * HD] = kept[which][head, seg - 1]
 
     def keys_of(which, seg, cols):
         if seg == 0:
@@ -339,12 +339,14 @@
     scores, weights, contexts = {}, {}, {}
     for turn in range(len(units) + LAGS[2]):
         if turn < len(units):
+            settle(0, *units[turn])
             scores[turn] = score(*units[turn])
         unit = turn - LAGS[0]
         if 0 <= unit < len(units) and units[unit][1] < count:
             weights[unit] = weigh(join(scores, unit))
         unit = turn - LAGS[1]
         if 0 <= unit < len(units):
+            settle(1, *units[unit])
             contexts[unit] = gather(*units[unit], unit)
         unit = turn - LAGS[2]
         if 0 <= unit < len(units) and units[unit][1] < count:

time: 54.2 us -> 54.2 us (level)
  no operation moved by 1% of the time
where the time goes in v1:
time: 54.2 us; the launch traced here: 54 us
  Pallas kernels  23.4 us (43%)
  starting transfers between devices  17.2 us (32%)
  waiting for transfers between devices  13.1 us (24%)
    pallas_call x4, Pallas kernels, project(): pl.pallas_call(functools.partial(project_kernel, parts=parts, stage=stage...  9.49 us
    ppermute x10, waiting for transfers between devices, swap(): return lax.ppermute(rows, axes, pairs)  8.6 us
    pallas_call x1, Pallas kernels, attend(): pl.pallas_call(functools.partial(attend_kernel, counts=(len(blocks), len(...  8.11 us
    ppermute x3, starting transfers between devices, attention(): arrived.append(lax.ppermute(parcels[away], 'seq', pairs))  7.04 us
    ppermute x10, starting transfers between devices, swap(): return lax.ppermute(rows, axes, pairs)  6.26 us
    ppermute x3, waiting for transfers between devices, attention(): arrived.append(lax.ppermute(parcels[away], 'seq', pairs))  4.51 us
    ppermute x1, starting transfers between devices, on_device_staged(): passed = lax.ppermute(tail, 'seq', ahead)  3.93 us
    pallas_call x1, Pallas kernels, hold(): pl.pallas_call(hold_kernel, out_shape=[jax.ShapeDtypeStruct(array.shape,...  3.49 us
  transfers between devices with their start and end apart: 14, of which 6 were waited for; matrix products, arithmetic and copies ran while one was open for 0% of the time, Pallas kernels for 24%

profile of v1, /device:TPU:0, one launch (start us, length us, event | category | flops | bytes accessed | tf_op | source)
XLA Modules:
  0.0 54.0 jit_solution(7517193620100877962)
XLA Ops:
  0.0 0.1 pad_add_fusion.place_ref
  0.1 1.9 %pack.1 = (bf16[328,128]{1,0:T(8,128)(2,1)S(1)}, bf16[328,128]{1,0:T(8,128)(2,1)S(1)}, bf16[328,128]{1,0:T(8,128)(2,1)S(1)}, bf16[328,128]{1,0:T(8,128)(2,1)S(1)}) custom-call(s32[20]{0:T(128)} %dest_hbm.1, s32[3]{0:T(128)S(1)} %pad_add_fusion.place_ref, bf16[20,8,1024]{2,1,0:T(8,128)(2,1)} %rows_hbm.1, f32[1,1024]{1,0:T(1,128)} %bitcast.4), custom_call_target="tpu_custom_call" | custom-call | tf_op jit(solution)/shard_map/pack/pallas_call | solution.py:82
  2.0 3.1 %collective-permute-start = (bf16[328,128]{1,0:T(8,128)(2,1)S(1)}, bf16[328,128]{1,0:T(8,128)(2,1)S(1)}, u32[]{:S(2)}, u32[]{:S(2)}) collective-permute-start(bf16[328,128]{1,0:T(8,128)(2,1)S(1)} %get-tuple-element.22), channel_id=1, source_target_pairs={{0,2},{2,4},{4,6},{6,0},{1,3},{3,5},{5,7},{7,1},{8,10},{10,12},{12... | collective-permute-start | bytes 251912 | tf_op jit(solution)/shard_map/ppermute | solution.py:470
  5.1 2.6 %collective-permute-start.1 = (bf16[328,128]{1,0:T(8,128)(2,1)S(1)}, bf16[328,128]{1,0:T(8,128)(2,1)S(1)}, u32[]{:S(2)}, u32[]{:S(2)}) collective-permute-start(bf16[328,128]{1,0:T(8,128)(2,1)S(1)} %get-tuple-element.23), channel_id=1, source_target_pairs={{0,4},{2,6},{4,0},{6,2},{1,5},{3,7},{5,1},{7,3},{8,12},{10,14},{12... | collective-permute-start | bytes 251912 | tf_op jit(solution)/shard_map/ppermute | solution.py:470
  7.7 1.3 %collective-permute-start.2 = (bf16[328,128]{1,0:T(8,128)(2,1)S(1)}, bf16[328,128]{1,0:T(8,128)(2,1)S(1)}, u32[]{:S(2)}, u32[]{:S(2)}) collective-permute-start(bf16[328,128]{1,0:T(8,128)(2,1)S(1)} %get-tuple-element.24), channel_id=1, source_target_pairs={{0,6},{2,0},{4,2},{6,4},{1,7},{3,1},{5,3},{7,5},{8,14},{10,8},{12,... | collective-permute-start | bytes 251912 | tf_op jit(solution)/shard_map/ppermute | solution.py:470
  9.1 1.1 %collective-permute-done.refs_1_ = bf16[328,128]{1,0:T(8,128)(2,1)S(1)} collective-permute-done((bf16[328,128]{1,0:T(8,128)(2,1)S(1)}, bf16[328,128]{1,0:T(8,128)(2,1)S(1)}, u32[]{:S(2)}, u32[]{:S(2)}) %collective-permute-start) | collective-permute-done | bytes 84000 | tf_op jit(solution)/shard_map/ppermute | solution.py:470
  10.2 3.1 %collective-permute-done.1.refs_2_ = bf16[328,128]{1,0:T(8,128)(2,1)S(1)} collective-permute-done((bf16[328,128]{1,0:T(8,128)(2,1)S(1)}, bf16[328,128]{1,0:T(8,128)(2,1)S(1)}, u32[]{:S(2)}, u32[]{:S(2)}) %collective-permute-start.1) | collective-permute-done | bytes 84000 | tf_op jit(solution)/shard_map/ppermute | solution.py:470
  13.3 0.2 collective-permute-done.2.refs_3_
  13.6 0.4 unpack.1
  14.0 3.9 %collective-permute-start.3 = (bf16[16,1024]{1,0:T(8,128)(2,1)S(1)}, bf16[16,1024]{1,0:T(8,128)(2,1)S(1)}, u32[]{:S(2)}, u32[]{:S(2)}) collective-permute-start(bf16[16,1024]{1,0:T(8,128)(2,1)S(1)} %get-tuple-element.25), channel_id=1, source_target_pairs={{0,2},{2,4},{4,6},{1,3},{3,5},{5,7},{8,10},{10,12},{12,14},{9,11},... | collective-permute-start | bytes 98312 | tf_op jit(solution)/shard_map/ppermute | solution.py:429
  17.9 3.5 %hold.1 = (bf16[1,1024,2048]{2,1,0:T(8,128)(2,1)S(1)}, bf16[1,1024,2048]{2,1,0:T(8,128)(2,1)S(1)}) custom-call(bf16[1,1024,2048]{2,1,0:T(8,128)(2,1)} %refs_0_.1, bf16[1,1024,2048]{2,1,0:T(8,128)(2,1)} %refs_1_.1), custom_call_target="tpu_custom_call" | custom-call | bytes 16777216 | tf_op jit(solution)/shard_map/hold/pallas_call | solution.py:189
  21.4 0.1 collective-permute-start.13
  21.5 1.6 %collective-permute-start.7 = (bf16[128,1024]{1,0:T(8,128)(2,1)S(1)}, bf16[128,1024]{1,0:T(8,128)(2,1)S(1)}, u32[]{:S(2)}, u32[]{:S(2)}) collective-permute-start(bf16[128,1024]{1,0:T(8,128)(2,1)S(1)} %get-tuple-element.28.refs_0_), channel_id=1, source_target_pairs={{0,1},{1,0},{8,24},{9,25},{16,17},{17,16},{24,8},{25,9},{2,3},{3,2... | collective-permute-start | bytes 786440 | tf_op jit(solution)/shard_map/ppermute | solution.py:412
  23.1 1.5 %collective-permute-start.11 = (bf16[128,1024]{1,0:T(8,128)(2,1)S(1)}, bf16[128,1024]{1,0:T(8,128)(2,1)S(1)}, u32[]{:S(2)}, u32[]{:S(2)}) collective-permute-start(bf16[128,1024]{1,0:T(8,128)(2,1)S(1)} %get-tuple-element.28.refs_0_), channel_id=1, source_target_pairs={{0,16},{1,17},{8,9},{9,8},{16,0},{17,1},{24,25},{25,24},{2,18},{3,... | collective-permute-start | bytes 786440 | tf_op jit(solution)/shard_map/ppermute | solution.py:412
  24.6 0.0 collective-permute-done.3
  24.6 0.5 collective-permute-start.4
  25.1 5.7 %collective-permute-done.4 = bf16[16,1024]{1,0:T(8,128)(2,1)S(1)} collective-permute-done((bf16[16,1024]{1,0:T(8,128)(2,1)S(1)}, bf16[16,1024]{1,0:T(8,128)(2,1)S(1)}, u32[]{:S(2)}, u32[]{:S(2)}) %collective-permute-start.4) | collective-permute-done | bytes 32800 | tf_op jit(solution)/shard_map/ppermute | solution.py:412
  30.8 1.5 %collective-permute-start.5 = (bf16[32,1024]{1,0:T(8,128)(2,1)S(1)}, bf16[32,1024]{1,0:T(8,128)(2,1)S(1)}, u32[]{:S(2)}, u32[]{:S(2)}) collective-permute-start(bf16[32,1024]{1,0:T(8,128)(2,1)S(1)} %pad_maximum_fusion), channel_id=1, source_target_pairs={{0,16},{1,17},{8,9},{9,8},{16,0},{17,1},{24,25},{25,24},{2,18},{3,... | collective-permute-start | bytes 196616 | tf_op jit(solution)/shard_map/ppermute | solution.py:412
  32.3 0.0 collective-permute-done.7.refs_0_
  32.3 0.5 collective-permute-start.8
  32.8 2.2 %collective-permute-done.5 = bf16[32,1024]{1,0:T(8,128)(2,1)S(1)} collective-permute-done((bf16[32,1024]{1,0:T(8,128)(2,1)S(1)}, bf16[32,1024]{1,0:T(8,128)(2,1)S(1)}, u32[]{:S(2)}, u32[]{:S(2)}) %collective-permute-start.5) | collective-permute-done | bytes 65568 | tf_op jit(solution)/shard_map/ppermute | solution.py:412
  35.1 0.0 collective-permute-start.6
  35.1 0.5 collective-permute-start.10
  35.6 0.0 collective-permute-done.11.refs_1_
  35.6 0.1 collective-permute-start.12
  35.6 0.0 collective-permute-done.13.refs_1_
  35.6 2.4 %project.4 = (bf16[16,8,128,128]{3,2,1,0:T(8,128)(2,1)S(1)}, bf16[16,8,128,128]{3,2,1,0:T(8,128)(2,1)S(1)}) custom-call(bf16[128,1024]{1,0:T(8,128)(2,1)S(1)} %get-tuple-element.28.refs_0_, bf16[128,1024]{1,0:T(8,128)(2,1)S(1)} %collective-permute-done.13.refs_1_, bf16[1,1024,2048]{2,1,0:T(8,128)(2,1)S(1)} %get-tuple-element.26.refs_2_, ...), custom_call_target="tpu_custom_call" | custom-call | flops 2147483648 | tf_op jit(solution)/shard_map/project/pallas_call | solution.py:239
  38.0 0.7 %collective-permute-done.8.refs_0_ = bf16[128,1024]{1,0:T(8,128)(2,1)S(1)} collective-permute-done((bf16[128,1024]{1,0:T(8,128)(2,1)S(1)}, bf16[128,1024]{1,0:T(8,128)(2,1)S(1)}, u32[]{:S(2)}, u32[]{:S(2)}) %collective-permute-start.8) | collective-permute-done | bytes 262176 | tf_op jit(solution)/shard_map/ppermute | solution.py:412
  38.7 0.0 collective-permute-start.9
  38.7 2.4 %project.5 = (bf16[16,8,128,128]{3,2,1,0:T(8,128)(2,1)S(1)}, bf16[16,8,128,128]{3,2,1,0:T(8,128)(2,1)S(1)}) custom-call(bf16[128,1024]{1,0:T(8,128)(2,1)S(1)} %collective-permute-done.7.refs_0_, bf16[128,1024]{1,0:T(8,128)(2,1)S(1)} %collective-permute-done.11.refs_1_, ...), custom_call_target="tpu_custom_call", output_to_operand_aliasing={{0}: (4, {}), {1}: (5, {})} | custom-call | flops 2147483648 | tf_op jit(solution)/shard_map/project/pallas_call | solution.py:239
  41.1 0.0 collective-permute-done.10.refs_0_
  41.1 0.0 collective-permute-done.12.refs_1_
  41.1 2.4 %project.6 = (bf16[16,8,128,128]{3,2,1,0:T(8,128)(2,1)S(1)}, bf16[16,8,128,128]{3,2,1,0:T(8,128)(2,1)S(1)}) custom-call(bf16[128,1024]{1,0:T(8,128)(2,1)S(1)} %collective-permute-done.10.refs_0_, bf16[128,1024]{1,0:T(8,128)(2,1)S(1)} %collective-permute-done.12.refs_1_, ...), custom_call_target="tpu_custom_call", output_to_operand_aliasing={{0}: (4, {}), {1}: (5, {})} | custom-call | flops 2147483648 | tf_op jit(solution)/shard_map/project/pallas_call | solution.py:239
  43.5 0.0 collective-permute-done.9.refs_1_
  43.5 0.0 copy-start
  43.5 2.4 %project.7 = (bf16[16,8,128,128]{3,2,1,0:T(8,128)(2,1)S(1)}, bf16[16,8,128,128]{3,2,1,0:T(8,128)(2,1)S(1)}) custom-call(bf16[128,1024]{1,0:T(8,128)(2,1)S(1)} %collective-permute-done.8.refs_0_, bf16[128,1024]{1,0:T(8,128)(2,1)S(1)} %collective-permute-done.9.refs_1_, ...), custom_call_target="tpu_custom_call", output_to_operand_aliasing={{0}: (4, {}), {1}: (5, {})} | custom-call | flops 2147483648 | tf_op jit(solution)/shard_map/project/pallas_call | solution.py:239
  45.9 0.0 collective-permute-done.6.refs_1_
  45.9 0.0 copy-done
  45.9 8.1 %attend.1 = bf16[1,512,2048]{2,1,0:T(8,128)(2,1)} custom-call(s32[3]{0:T(128)S(1)} %pad_add_fusion.place_ref, bf16[64,1024]{1,0:T(8,128)(2,1)S(1)} %constant_dynamic-update-slice_fusion.refs_0_, bf16[64,1024]{1,0:T(8,128)(2,1)S(1)} %collective-permute-done.6.refs_1_, bf16[1,1024,2048]{2,1,0:T(8,128)(2,1)S(1)} %get-tuple-element.26.refs_2_, ...), custom_call_target="tpu_custom_call" | custom-call | tf_op jit(solution)/shard_map/attend/pallas_call | solution.py:374
  (4 shorter events, 0.0 us)
Async XLA Ops:
  2.0 8.2 %collective-permute-start = (bf16[328,128]{1,0:T(8,128)(2,1)S(1)}, bf16[328,128]{1,0:T(8,128)(2,1)S(1)}, u32[]{:S(2)}, u32[]{:S(2)}) collective-permute-start(bf16[328,128]{1,0:T(8,128)(2,1)S(1)} %get-tuple-element.22), channel_id=1, source_target_pairs={{0,2},{2,4},{4,6},{6,0},{1,3},{3,5},{5,7},{7,1},{8,10},{10,12},{12... | collective-permute-start | bytes 251912 | tf_op jit(solution)/shard_map/ppermute | solution.py:470
  5.1 8.2 %collective-permute-start.1 = (bf16[328,128]{1,0:T(8,128)(2,1)S(1)}, bf16[328,128]{1,0:T(8,128)(2,1)S(1)}, u32[]{:S(2)}, u32[]{:S(2)}) collective-permute-start(bf16[328,128]{1,0:T(8,128)(2,1)S(1)} %get-tuple-element.23), channel_id=1, source_target_pairs={{0,4},{2,6},{4,0},{6,2},{1,5},{3,7},{5,1},{7,3},{8,12},{10,14},{12... | collective-permute-start | bytes 251912 | tf_op jit(solution)/shard_map/ppermute | solution.py:470
  7.7 5.9 %collective-permute-start.2 = (bf16[328,128]{1,0:T(8,128)(2,1)S(1)}, bf16[328,128]{1,0:T(8,128)(2,1)S(1)}, u32[]{:S(2)}, u32[]{:S(2)}) collective-permute-start(bf16[328,128]{1,0:T(8,128)(2,1)S(1)} %get-tuple-element.24), channel_id=1, source_target_pairs={{0,6},{2,0},{4,2},{6,4},{1,7},{3,1},{5,3},{7,5},{8,14},{10,8},{12,... | collective-permute-start | bytes 251912 | tf_op jit(solution)/shard_map/ppermute | solution.py:470
  14.0 10.6 %collective-permute-start.3 = (bf16[16,1024]{1,0:T(8,128)(2,1)S(1)}, bf16[16,1024]{1,0:T(8,128)(2,1)S(1)}, u32[]{:S(2)}, u32[]{:S(2)}) collective-permute-start(bf16[16,1024]{1,0:T(8,128)(2,1)S(1)} %get-tuple-element.25), channel_id=1, source_target_pairs={{0,2},{2,4},{4,6},{1,3},{3,5},{5,7},{8,10},{10,12},{12,14},{9,11},... | collective-permute-start | bytes 98312 | tf_op jit(solution)/shard_map/ppermute | solution.py:429
  21.4 14.2 %collective-permute-start.13 = (bf16[128,1024]{1,0:T(8,128)(2,1)S(1)}, bf16[128,1024]{1,0:T(8,128)(2,1)S(1)}, u32[]{:S(2)}, u32[]{:S(2)}) collective-permute-start(bf16[128,1024]{1,0:T(8,128)(2,1)S(1)} %get-tuple-element.28.refs_0_), channel_id=1, source_target_pairs={{0,8},{1,9},{8,0},{9,1},{16,24},{17,25},{24,16},{25,17},{2,10},{3,... | collective-permute-start | bytes 786440 | tf_op jit(solution)/shard_map/ppermute | solution.py:412
  21.5 10.8 %collective-permute-start.7 = (bf16[128,1024]{1,0:T(8,128)(2,1)S(1)}, bf16[128,1024]{1,0:T(8,128)(2,1)S(1)}, u32[]{:S(2)}, u32[]{:S(2)}) collective-permute-start(bf16[128,1024]{1,0:T(8,128)(2,1)S(1)} %get-tuple-element.28.refs_0_), channel_id=1, source_target_pairs={{0,1},{1,0},{8,24},{9,25},{16,17},{17,16},{24,8},{25,9},{2,3},{3,2... | collective-permute-start | bytes 786440 | tf_op jit(solution)/shard_map/ppermute | solution.py:412
  23.1 12.5 %collective-permute-start.11 = (bf16[128,1024]{1,0:T(8,128)(2,1)S(1)}, bf16[128,1024]{1,0:T(8,128)(2,1)S(1)}, u32[]{:S(2)}, u32[]{:S(2)}) collective-permute-start(bf16[128,1024]{1,0:T(8,128)(2,1)S(1)} %get-tuple-element.28.refs_0_), channel_id=1, source_target_pairs={{0,16},{1,17},{8,9},{9,8},{16,0},{17,1},{24,25},{25,24},{2,18},{3,... | collective-permute-start | bytes 786440 | tf_op jit(solution)/shard_map/ppermute | solution.py:412
  24.6 6.2 %collective-permute-start.4 = (bf16[16,1024]{1,0:T(8,128)(2,1)S(1)}, bf16[16,1024]{1,0:T(8,128)(2,1)S(1)}, u32[]{:S(2)}, u32[]{:S(2)}) collective-permute-start(bf16[16,1024]{1,0:T(8,128)(2,1)S(1)} %collective-permute-done.3), channel_id=1, source_target_pairs={{0,1},{1,0},{8,24},{9,25},{16,17},{17,16},{24,8},{25,9},{2,3},{3,2... | collective-permute-start | bytes 98312 | tf_op jit(solution)/shard_map/ppermute | solution.py:412
  30.8 4.3 %collective-permute-start.5 = (bf16[32,1024]{1,0:T(8,128)(2,1)S(1)}, bf16[32,1024]{1,0:T(8,128)(2,1)S(1)}, u32[]{:S(2)}, u32[]{:S(2)}) collective-permute-start(bf16[32,1024]{1,0:T(8,128)(2,1)S(1)} %pad_maximum_fusion), channel_id=1, source_target_pairs={{0,16},{1,17},{8,9},{9,8},{16,0},{17,1},{24,25},{25,24},{2,18},{3,... | collective-permute-start | bytes 196616 | tf_op jit(solution)/shard_map/ppermute | solution.py:412
  32.3 6.4 %collective-permute-start.8 = (bf16[128,1024]{1,0:T(8,128)(2,1)S(1)}, bf16[128,1024]{1,0:T(8,128)(2,1)S(1)}, u32[]{:S(2)}, u32[]{:S(2)}) collective-permute-start(bf16[128,1024]{1,0:T(8,128)(2,1)S(1)} %collective-permute-done.7.refs_0_), channel_id=1, source_target_pairs={{0,16},{1,17},{8,9},{9,8},{16,0},{17,1},{24,25},{25,24},{2,18},{3,... | collective-permute-start | bytes 786440 | tf_op jit(solution)/shard_map/ppermute | solution.py:412
  35.1 10.8 %collective-permute-start.6 = (bf16[64,1024]{1,0:T(8,128)(2,1)S(1)}, bf16[64,1024]{1,0:T(8,128)(2,1)S(1)}, u32[]{:S(2)}, u32[]{:S(2)}) collective-permute-start(bf16[64,1024]{1,0:T(8,128)(2,1)S(1)} %constant_dynamic-update-slice_fusion.refs_0_), channel_id=1, source_target_pairs={{0,8},{1,9},{8,0},{9,1},{16,24},{17,25},{24,16},{25,17},{2,10},{3,... | collective-permute-start | bytes 393224 | tf_op jit(solution)/shard_map/ppermute | solution.py:412
  35.1 6.0 %collective-permute-start.10 = (bf16[128,1024]{1,0:T(8,128)(2,1)S(1)}, bf16[128,1024]{1,0:T(8,128)(2,1)S(1)}, u32[]{:S(2)}, u32[]{:S(2)}) collective-permute-start(bf16[128,1024]{1,0:T(8,128)(2,1)S(1)} %collective-permute-done.7.refs_0_), channel_id=1, source_target_pairs={{0,8},{1,9},{8,0},{9,1},{16,24},{17,25},{24,16},{25,17},{2,10},{3,... | collective-permute-start | bytes 786440 | tf_op jit(solution)/shard_map/ppermute | solution.py:412
  35.6 5.5 %collective-permute-start.12 = (bf16[128,1024]{1,0:T(8,128)(2,1)S(1)}, bf16[128,1024]{1,0:T(8,128)(2,1)S(1)}, u32[]{:S(2)}, u32[]{:S(2)}) collective-permute-start(bf16[128,1024]{1,0:T(8,128)(2,1)S(1)} %collective-permute-done.11.refs_1_), channel_id=1, source_target_pairs={{0,8},{1,9},{8,0},{9,1},{16,24},{17,25},{24,16},{25,17},{2,10},{3,... | collective-permute-start | bytes 786440 | tf_op jit(solution)/shard_map/ppermute | solution.py:412
  38.7 4.8 %collective-permute-start.9 = (bf16[128,1024]{1,0:T(8,128)(2,1)S(1)}, bf16[128,1024]{1,0:T(8,128)(2,1)S(1)}, u32[]{:S(2)}, u32[]{:S(2)}) collective-permute-start(bf16[128,1024]{1,0:T(8,128)(2,1)S(1)} %collective-permute-done.8.refs_0_), channel_id=1, source_target_pairs={{0,8},{1,9},{8,0},{9,1},{16,24},{17,25},{24,16},{25,17},{2,10},{3,... | collective-permute-start | bytes 786440 | tf_op jit(solution)/shard_map/ppermute | solution.py:412
  43.5 2.4 %copy-start = (bf16[1,512,2048]{2,1,0:T(8,128)(2,1)S(1)}, bf16[1,512,2048]{2,1,0:T(8,128)(2,1)}, u32[]{:S(2)}) copy-start(bf16[1,512,2048]{2,1,0:T(8,128)(2,1)} %refs_4_.1) | copy-start | bytes 6291460
